TPU v7x, 32 devices: a whole 2x2x4 slice. The times are simulated.
32 devices in a mesh: groups: 2 (over x), month: 16 (over z, y, core).
Axes of the slice: x: 2, y: 2, z: 4, core: 2. Of those that a mesh axis runs over, the one named last changes fastest.
Arguments:
- shocks: float32 [512, 4096], P('month', 'groups'), parts along dimension 1, may hold values from -6 to 6
- long_mean: float32 [512], P('month'), may hold values from 0 to 0.08
- reversion: float32 [4096], P('groups'), parts along dimension 0, may hold values from 0.1 to 1
- volatility: float32 [4096], P('groups'), parts along dimension 0, may hold values from 0.004 to 0.015
- start_rate: float32 [4096], P('groups'), parts along dimension 0, may hold values from 0 to 0.06
- cash_flows: bfloat16 [3, 512, 24576], P(None, 'month', 'groups'), parts along dimension 2, may hold values from -0.5 to 0.5
Outputs:
- present: bfloat16 [3, 24576, 2048], P(None, ('groups', 'month')), parts along dimension 1
There are 2 independent parts, one for each index of `groups`. A program takes and returns all parts, laid end to end along the dimension named above; an argument that names none is the same for every part. Nothing has to cross between parts.
All inputs are finite; a program needn't handle non-finite values.
Results may differ from a plain program's by a relative error of at most 0.0049.
Values may be sent and summed in bfloat16 or wider, within the bound.
A program may use at most 192 MiB of HBM per device.

v0:
```python
import math
import jax
import jax.numpy as jnp
from jax import lax
from jax.sharding import PartitionSpec as P

month_step = 1.0 / 12.0
root_step = math.sqrt(1.0 / 12.0)
risk_price = 0.15
price_scale = risk_price * math.sqrt(12.0)
price_drift = 0.5 * risk_price * risk_price


def prefix(part, axis, combine, identity):
    place = lax.axis_index(axis)
    gathered = jax.tree.map(lambda a: lax.all_gather(a, axis), part)
    state = jax.tree.map(lambda a, e: jnp.zeros_like(a) + jnp.asarray(e, a.dtype), part, identity)

    def one(hop, state):
        return combine(
            state, jax.tree.map(lambda a: lax.dynamic_index_in_dim(a, hop, 0, False), gathered)
        )

    return lax.fori_loop(0, place, one, state)


def compose(earlier, later):
    return (
        later[0] * earlier[0],
        later[0] * earlier[1] + later[1],
        earlier[2] + later[2] * earlier[0],
        earlier[3] + later[3] + later[2] * earlier[1],
    )


def month_maps(shocks, long_mean, reversion, volatility):
    persist = 1.0 - reversion * month_step
    drive = (reversion * month_step)[None, :] * long_mean[:, None] + (volatility * root_step)[
        None, :
    ] * shocks
    factor = jnp.broadcast_to(persist[None, :], drive.shape)
    extra = drive + price_scale * shocks + price_drift
    return lax.associative_scan(compose, (factor, drive, factor, extra), axis=0)


def discount_from(maps, rate_in, total_in):
    total = total_in[None, :] + maps[2] * rate_in[None, :] + maps[3]
    return jnp.exp(-month_step * total).astype(jnp.bfloat16)


def time_discount(shocks, long_mean, reversion, volatility, start_rate):
    maps = month_maps(shocks, long_mean, reversion, volatility)
    block = tuple((member[-1] for member in maps))
    unit_row = jnp.ones_like(start_rate)
    zero_row = jnp.zeros_like(start_rate)
    before = prefix(block, "month", compose, (unit_row, zero_row, zero_row, zero_row))
    rate_in = before[0] * start_rate + before[1]
    total_in = before[2] * start_rate + before[3]
    return discount_from(maps, rate_in, total_in)


def contract(flows, discount):
    blocks = []
    for leg_index in range(flows.shape[0]):
        value = lax.dot_general(
            flows[leg_index], discount, (((0,), (0,)), ((), ())), preferred_element_type=jnp.float32
        )
        blocks.append(value.astype(jnp.bfloat16))
    return jnp.stack(blocks)


def local(shocks, long_mean, reversion, volatility, start_rate, cash_flows):
    own_flows = lax.all_to_all(cash_flows, "month", split_axis=2, concat_axis=1, tiled=True)
    discount = time_discount(shocks, long_mean, reversion, volatility, start_rate)
    every_month = lax.all_gather(discount, "month", axis=0, tiled=True)
    return contract(own_flows, every_month)


def solution(mesh):
    placed = (
        P("month", "groups"),
        P("month"),
        P("groups"),
        P("groups"),
        P("groups"),
        P(None, "month", "groups"),
    )
    return jax.shard_map(
        local,
        mesh=mesh,
        in_specs=placed,
        out_specs=P(None, ("groups", "month"), None),
        check_vma=False,
    )
```

profile of v0, /device:TPU:0, one launch (start us, length us, event | category | flops | bytes accessed | tf_op | source)
XLA Modules:
  0.0 273.4 jit_solution(5829222085009719674)
XLA Ops:
  6.5 15.3 %copy.13 = bf16[3,32,12288]{1,0,2:T(4,128)(2,1)} copy(bf16[3,32,12288]{2,1,0:T(8,128)(2,1)} %param.13) | data formatting | bytes 4718592 | tf_op args[5]
  21.8 15.7 %reshape.39 = bf16[16,2,36864]{2,1,0:T(2,128)(2,1)} reshape(bf16[12288,3,32]{2,1,0:T(4,128)(2,1)} %bitcast.69) | data formatting | bytes 4718592
  37.5 7.6 %all-to-all-start = ((bf16[16,2,36864]{2,1,0:T(2,128)(2,1)}), bf16[16,2,36864]{2,1,0:T(2,128)(2,1)S(1)}, u32[]{:S(2)}, u32[]{:S(2)}) async-start(bf16[16,2,36864]{2,1,0:T(2,128)(2,1)} %reshape.39), calls=%async_computation | async-start | bytes 4718592 | tf_op jit(solution)/shard_map/all_to_all | solution.py:73
  51.3 0.7 pad_maximum_fusion.8
  54.2 0.9 pad_maximum_fusion.7
  55.1 0.9 pad.153
  56.0 0.9 add_add_fusion.2
  57.1 43.2 %all-gather.2 = f32[16,1,2048]{2,1,0:T(1,128)S(1)} all-gather(f32[1,1,2048]{2,1,0:T(1,128)S(1)} %add_bitcast_fusion.1), channel_id=1, replica_groups=mesh['groups'=2,'month'=16] {'month'}, dimensions={0}, use_global_device_ids=true | all-gather | bytes 139264 | tf_op jit(solution)/shard_map/all_gather | solution.py:16
  101.8 1.0 pad.165
  102.8 28.5 %all-gather.3 = f32[16,1,2048]{2,1,0:T(1,128)S(1)} all-gather(f32[1,1,2048]{2,1,0:T(1,128)S(1)} %add_bitcast_fusion), channel_id=1, replica_groups=mesh['groups'=2,'month'=16] {'month'}, dimensions={0}, use_global_device_ids=true | all-gather | bytes 139264 | tf_op jit(solution)/shard_map/all_gather | solution.py:16
  132.0 2.3 pad.299
  134.4 1.4 pad.301
  135.8 0.9 add_bitcast_fusion.2
  136.7 17.8 %all-gather.1 = f32[16,1,2048]{2,1,0:T(1,128)S(1)} all-gather(f32[1,1,2048]{2,1,0:T(1,128)S(1)} %get-tuple-element.132), channel_id=1, replica_groups=mesh['groups'=2,'month'=16] {'month'}, dimensions={0}, use_global_device_ids=true | all-gather | bytes 139264 | tf_op jit(solution)/shard_map/all_gather | solution.py:16
  155.2 19.1 %all-gather = f32[16,1,2048]{2,1,0:T(1,128)S(1)} all-gather(f32[1,1,2048]{2,1,0:T(1,128)S(1)} %get-tuple-element.133), channel_id=1, replica_groups=mesh['groups'=2,'month'=16] {'month'}, dimensions={0}, use_global_device_ids=true | all-gather | bytes 139264 | tf_op jit(solution)/shard_map/all_gather | solution.py:16
  175.2 0.7 exponential_convert_fusion
  176.0 11.8 %reshape.40 = bf16[12288,3,32]{2,1,0:T(4,128)(2,1)} reshape(bf16[16,2,36864]{2,1,0:T(2,128)(2,1)S(1)} %all-to-all-done) | data formatting | bytes 4718592
  187.7 11.7 %copy.19 = bf16[3,32,16,768]{3,2,1,0:T(8,128)(2,1)S(1)} copy(bf16[3,32,16,768]{1,0,3,2:T(4,128)(2,1)} %bitcast.68) | data formatting | bytes 4718592 | tf_op jit(solution)/shard_map/all_to_all | solution.py:73
  200.3 41.7 %all-gather.6.cloned.1.call-done = bf16[512,2048]{1,0:T(8,128)(2,1)} async-done(((bf16[32,2048]{1,0:T(8,128)(2,1)}), bf16[512,2048]{1,0:T(8,128)(2,1)}) %all-gather.6.cloned.1.call-update) | async-done | bytes 2097168 | tf_op jit(solution)/shard_map/all_gather | solution.py:75
  242.0 3.6 %fusion.1 = bf16[1,768,2048]{1,2,0:T(8,128)(2,1)S(1)} fusion(bf16[512,2048]{1,0:T(8,128)(2,1)} %all-gather.6.cloned.1.call-done, bf16[512,768]{1,0:T(8,128)(2,1)S(1)} %bitcast.77), kind=kOutput, calls=%fused_computation.12 | convolution fusion | flops 1612185600 | bytes 6029312 | tf_op jit(solution)/shard_map/dot_general | solution.py:65
  245.6 1.9 fusion.2
  247.5 1.9 fusion
  249.4 4.6 %pad_maximum_fusion = bf16[3,768,2048]{1,2,0:T(8,128)(2,1)} fusion(bf16[1,768,2048]{1,2,0:T(8,128)(2,1)S(1)} %fusion.2, bf16[1,768,2048]{1,2,0:T(8,128)(2,1)S(1)} %fusion.1, bf16[1,768,2048]{1,2,0:T(8,128)(2,1)S(1)} %fusion), kind=kLoop, calls=%fused_computation.7 | loop fusion | flops 9437184 | bytes 18874368 | tf_op jit(solution)/shard_map/stack | solution.py:69
  253.9 12.6 %copy.18 = bf16[3,768,2048]{2,1,0:T(8,128)(2,1)} copy(bf16[3,768,2048]{1,2,0:T(8,128)(2,1)} %pad_maximum_fusion) | data formatting | bytes 18874368 | tf_op jit(solution)/shard_map/stack | solution.py:69
  (123 shorter events, 12.7 us)
Async XLA Ops:
  37.5 7.6 %copy-start.2 = (f32[2048]{0:T(1024)S(1)}, f32[2048]{0:T(1024)}, u32[]{:S(2)}) copy-start(f32[2048]{0:T(1024)} %param.10) | copy-start | bytes 24580
  37.5 7.6 %copy-start.3 = (f32[2048]{0:T(1024)S(1)}, f32[2048]{0:T(1024)}, u32[]{:S(2)}) copy-start(f32[2048]{0:T(1024)} %param.11) | copy-start | bytes 24580
  37.5 7.7 %copy-start = (f32[32,2048]{1,0:T(8,128)S(1)}, f32[32,2048]{1,0:T(8,128)}, u32[]{:S(2)}) copy-start(f32[32,2048]{1,0:T(8,128)} %param.8) | copy-start | bytes 786436
  37.5 7.7 %copy-start.4 = (f32[32]{0:T(128)S(1)}, f32[32]{0:T(128)}, u32[]{:S(2)}) copy-start(f32[32]{0:T(128)} %param.9) | copy-start | bytes 388
  37.5 138.4 %all-to-all-start = ((bf16[16,2,36864]{2,1,0:T(2,128)(2,1)}), bf16[16,2,36864]{2,1,0:T(2,128)(2,1)S(1)}, u32[]{:S(2)}, u32[]{:S(2)}) async-start(bf16[16,2,36864]{2,1,0:T(2,128)(2,1)} %reshape.39), calls=%async_computation | async-start | bytes 4718592 | tf_op jit(solution)/shard_map/all_to_all | solution.py:73
  45.1 196.9 %all-gather.6.cloned.1.call-start = ((), (), s32[]{:S(2)}) async-start(), calls=%async_computation.1 | async-start | bytes 2228224 | tf_op jit(solution)/shard_map/all_gather | solution.py:75
  56.0 119.2 %copy-start.1 = (f32[2048]{0:T(1024)S(1)}, f32[2048]{0:T(1024)}, u32[]{:S(2)}) copy-start(f32[2048]{0:T(1024)} %param.12) | copy-start | bytes 24580
  242.0 3.6 %copy-start.5 = (bf16[512,2048]{1,0:T(8,128)(2,1)S(1)}, bf16[512,2048]{1,0:T(8,128)(2,1)}, u32[]{:S(2)}) copy-start(bf16[512,2048]{1,0:T(8,128)(2,1)} %all-gather.6.cloned.1.call-done) | copy-start | bytes 6291460
Sparse Core Ops, SparseCore 0:
  176.1 65.8 all-gather.5
where the time goes:
time: 277 us; the launch traced here: 273 us
  blocking collectives  109 us (39%)
  local copies, waits for them, and re-layouts  79.5 us (29%)
  waiting for transfers between devices  41.7 us (15%)
  other arithmetic  14.3 us (5%)
  between operations  14.1 us (5%)
  starting transfers between devices  7.6 us (3%)
  matrix products  7.31 us (3%)
    all_gather x4, blocking collectives, prefix(): gathered = jax.tree.map(lambda a: lax.all_gather(a, axis), part)  109 us
    unnamed x21, local copies, waits for them, and re-layouts  49.3 us
    all_gather x1, waiting for transfers between devices, local(): every_month = lax.all_gather(discount, 'month', axis=0, tiled=True)  41.7 us
    another operation x1, local copies, waits for them, and re-layouts, contract(): return jnp.stack(blocks)  12.6 us
    all_to_all x1, local copies, waits for them, and re-layouts, local(): lax.all_to_all(cash_flows, 'month', split_axis=2, concat_axis=1, tiled=True)  11.7 us
    all_to_all x1, starting transfers between devices, local(): lax.all_to_all(cash_flows, 'month', split_axis=2, concat_axis=1, tiled=True)  7.56 us
    dot_general x3, matrix products, contract(): lax.dot_general(flows[leg_index], discount, (((0,), (0,)), ((), ())), pre...  7.31 us
  transfers between devices with their start and end apart: 2, of which 1 were waited for; matrix products, arithmetic and copies ran while one was open for 17% of the time, Pallas kernels for 0%

commit v1 on v0

--- a/solution.py
+++ b/solution.py
@@ -9,6 +9,27 @@
 risk_price = 0.15
 price_scale = risk_price * math.sqrt(12.0)
 price_drift = 0.5 * risk_price * risk_price
+
+
+def collect(array, axis, dim):
+    size, index, rows = (lax.axis_size(axis), lax.axis_index(axis), array.shape[dim])
+    right = [(i, (i + 1) % size) for i in range(size)]
+    left = [(i, (i - 1) % size) for i in range(size)]
+    out = jnp.zeros((*array.shape[:dim], size * rows, *array.shape[dim + 1 :]), array.dtype)
+    out = lax.dynamic_update_slice_in_dim(out, array, index * rows, axis=dim)
+    from_left = from_right = array
+    halfway = size // 2
+    for step in range(1, halfway + 1):
+        from_left = lax.ppermute(from_left, axis, right)
+        out = lax.dynamic_update_slice_in_dim(
+            out, from_left, (index - step) % size * rows, axis=dim
+        )
+        if step < size - halfway:
+            from_right = lax.ppermute(from_right, axis, left)
+            out = lax.dynamic_update_slice_in_dim(
+                out, from_right, (index + step) % size * rows, axis=dim
+            )
+    return out
 
 
 def prefix(part, axis, combine, identity):
@@ -72,7 +93,7 @@
 def local(shocks, long_mean, reversion, volatility, start_rate, cash_flows):
     own_flows = lax.all_to_all(cash_flows, "month", split_axis=2, concat_axis=1, tiled=True)
     discount = time_discount(shocks, long_mean, reversion, volatility, start_rate)
-    every_month = lax.all_gather(discount, "month", axis=0, tiled=True)
+    every_month = collect(discount, "month", 0)
     return contract(own_flows, every_month)
 
 

time: 277 us -> 306 us (1.10)
  starting transfers between devices: 7.6 us -> 62 us
  waiting for transfers between devices: 41.7 us -> 16.7 us
  between operations: 14.1 us -> 0.75 us
  local copies, waits for them, and re-layouts: 79.5 us -> 91 us
    ppermute x0 -> x15, starting transfers between devices: none -> 54.5 us  [the longest x7 52.3 us: collect(): from_right = lax.ppermute(from_right, axis, left)]
    all_gather x1 -> x0, waiting for transfers between devices: 41.7 us -> none  [local(): every_month = lax.all_gather(discount, 'month', axis=0, tiled=True)]
    ppermute x0 -> x15, waiting for transfers between devices: none -> 16.7 us  [the longest x8 16.7 us: collect(): from_left = lax.ppermute(from_left, axis, right)]
    dynamic_update_slice x0 -> x15, local copies, waits for them, and re-layouts: none -> 9.93 us  [the longest x8 5.32 us: collect(): lax.dynamic_update_slice_in_dim(out, from_left, (index - step) % size * r...]
    unnamed x21 -> x25, local copies, waits for them, and re-layouts: 49.3 us -> 49.3 us
  transfers between devices with their start and end apart: 2 -> 16, of which waited for: 1 -> 8; matrix products, arithmetic and copies ran while one was open for 17% -> 10% of each run, Pallas kernels for 0% -> 0%
where the time goes in v1:
time: 306 us; the launch traced here: 303 us
  blocking collectives  110 us (36%)
  local copies, waits for them, and re-layouts  91 us (30%)
  starting transfers between devices  62 us (20%)
  waiting for transfers between devices  16.7 us (5%)
  other arithmetic  12.1 us (4%)
  matrix products  10.3 us (3%)
    all_gather x4, blocking collectives, prefix(): gathered = jax.tree.map(lambda a: lax.all_gather(a, axis), part)  110 us
    ppermute x7, starting transfers between devices, collect(): from_right = lax.ppermute(from_right, axis, left)  52.3 us
    unnamed x25, local copies, waits for them, and re-layouts  49.3 us
    ppermute x8, waiting for transfers between devices, collect(): from_left = lax.ppermute(from_left, axis, right)  16.7 us
    another operation x1, local copies, waits for them, and re-layouts, contract(): return jnp.stack(blocks)  12.6 us
    all_to_all x1, local copies, waits for them, and re-layouts, local(): lax.all_to_all(cash_flows, 'month', split_axis=2, concat_axis=1, tiled=True)  11.7 us
    dot_general x3, matrix products, contract(): lax.dot_general(flows[leg_index], discount, (((0,), (0,)), ((), ())), pre...  10.3 us
    all_to_all x1, starting transfers between devices, local(): lax.all_to_all(cash_flows, 'month', split_axis=2, concat_axis=1, tiled=True)  7.56 us
  transfers between devices with their start and end apart: 16, of which 8 were waited for; matrix products, arithmetic and copies ran while one was open for 10% of the time, Pallas kernels for 0%

profile of v1, /device:TPU:0, one launch (start us, length us, event | category | flops | bytes accessed | tf_op | source)
XLA Modules:
  0.0 303.0 jit_solution(12102791559364226463)
XLA Ops:
  0.0 15.3 %copy.13 = bf16[3,32,12288]{1,0,2:T(4,128)(2,1)} copy(bf16[3,32,12288]{2,1,0:T(8,128)(2,1)} %param.13) | data formatting | bytes 4718592 | tf_op args[5]
  15.3 15.7 %reshape.39 = bf16[16,2,36864]{2,1,0:T(2,128)(2,1)} reshape(bf16[12288,3,32]{2,1,0:T(4,128)(2,1)} %bitcast.69) | data formatting | bytes 4718592
  31.0 7.6 %all-to-all-start = ((bf16[16,2,36864]{2,1,0:T(2,128)(2,1)}), bf16[16,2,36864]{2,1,0:T(2,128)(2,1)S(1)}, u32[]{:S(2)}, u32[]{:S(2)}) async-start(bf16[16,2,36864]{2,1,0:T(2,128)(2,1)} %reshape.39), calls=%async_computation | async-start | bytes 4718592 | tf_op jit(solution)/shard_map/all_to_all | solution.py:94
  49.0 44.8 %all-gather.2 = f32[16,1,2048]{2,1,0:T(1,128)S(1)} all-gather(f32[1,1,2048]{2,1,0:T(1,128)S(1)} %add_bitcast_fusion.1), channel_id=1, replica_groups=mesh['groups'=2,'month'=16] {'month'}, dimensions={0}, use_global_device_ids=true | all-gather | bytes 139264 | tf_op jit(solution)/shard_map/all_gather | solution.py:37
  95.6 28.5 %all-gather.3 = f32[16,1,2048]{2,1,0:T(1,128)S(1)} all-gather(f32[1,1,2048]{2,1,0:T(1,128)S(1)} %add_bitcast_fusion), channel_id=1, replica_groups=mesh['groups'=2,'month'=16] {'month'}, dimensions={0}, use_global_device_ids=true | all-gather | bytes 139264 | tf_op jit(solution)/shard_map/all_gather | solution.py:37
  124.8 2.3 pad.299
  129.5 17.8 %all-gather.1 = f32[16,1,2048]{2,1,0:T(1,128)S(1)} all-gather(f32[1,1,2048]{2,1,0:T(1,128)S(1)} %get-tuple-element.148), channel_id=1, replica_groups=mesh['groups'=2,'month'=16] {'month'}, dimensions={0}, use_global_device_ids=true | all-gather | bytes 139264 | tf_op jit(solution)/shard_map/all_gather | solution.py:37
  147.9 19.1 %all-gather = f32[16,1,2048]{2,1,0:T(1,128)S(1)} all-gather(f32[1,1,2048]{2,1,0:T(1,128)S(1)} %get-tuple-element.149), channel_id=1, replica_groups=mesh['groups'=2,'month'=16] {'month'}, dimensions={0}, use_global_device_ids=true | all-gather | bytes 139264 | tf_op jit(solution)/shard_map/all_gather | solution.py:37
  172.3 25.6 %collective-permute-start.1 = (bf16[32,2048]{1,0:T(8,128)(2,1)S(1)}, bf16[32,2048]{1,0:T(8,128)(2,1)S(1)}, u32[]{:S(2)}, u32[]{:S(2)}) collective-permute-start(bf16[32,2048]{1,0:T(8,128)(2,1)S(1)} %get-tuple-element.86), channel_id=1, source_target_pairs={{0,15},{1,0},{2,1},{3,2},{4,3},{5,4},{6,5},{7,6},{8,7},{9,8},{10,9... | collective-permute-start | bytes 393224 | tf_op jit(solution)/shard_map/ppermute | solution.py:28
  197.8 2.6 collective-permute-done
  200.5 4.5 %collective-permute-start.3 = (bf16[32,2048]{1,0:T(8,128)(2,1)S(1)}, bf16[32,2048]{1,0:T(8,128)(2,1)S(1)}, u32[]{:S(2)}, u32[]{:S(2)}) collective-permute-start(bf16[32,2048]{1,0:T(8,128)(2,1)S(1)} %collective-permute-done.1), channel_id=1, source_target_pairs={{0,15},{1,0},{2,1},{3,2},{4,3},{5,4},{6,5},{7,6},{8,7},{9,8},{10,9... | collective-permute-start | bytes 393224 | tf_op jit(solution)/shard_map/ppermute | solution.py:28
  207.7 4.4 %collective-permute-start.5 = (bf16[32,2048]{1,0:T(8,128)(2,1)S(1)}, bf16[32,2048]{1,0:T(8,128)(2,1)S(1)}, u32[]{:S(2)}, u32[]{:S(2)}) collective-permute-start(bf16[32,2048]{1,0:T(8,128)(2,1)S(1)} %collective-permute-done.3), channel_id=1, source_target_pairs={{0,15},{1,0},{2,1},{3,2},{4,3},{5,4},{6,5},{7,6},{8,7},{9,8},{10,9... | collective-permute-start | bytes 393224 | tf_op jit(solution)/shard_map/ppermute | solution.py:28
  214.8 4.4 %collective-permute-start.7 = (bf16[32,2048]{1,0:T(8,128)(2,1)S(1)}, bf16[32,2048]{1,0:T(8,128)(2,1)S(1)}, u32[]{:S(2)}, u32[]{:S(2)}) collective-permute-start(bf16[32,2048]{1,0:T(8,128)(2,1)S(1)} %collective-permute-done.5), channel_id=1, source_target_pairs={{0,15},{1,0},{2,1},{3,2},{4,3},{5,4},{6,5},{7,6},{8,7},{9,8},{10,9... | collective-permute-start | bytes 393224 | tf_op jit(solution)/shard_map/ppermute | solution.py:28
  222.0 4.4 %collective-permute-start.9 = (bf16[32,2048]{1,0:T(8,128)(2,1)S(1)}, bf16[32,2048]{1,0:T(8,128)(2,1)S(1)}, u32[]{:S(2)}, u32[]{:S(2)}) collective-permute-start(bf16[32,2048]{1,0:T(8,128)(2,1)S(1)} %collective-permute-done.7), channel_id=1, source_target_pairs={{0,15},{1,0},{2,1},{3,2},{4,3},{5,4},{6,5},{7,6},{8,7},{9,8},{10,9... | collective-permute-start | bytes 393224 | tf_op jit(solution)/shard_map/ppermute | solution.py:28
  229.2 4.4 %collective-permute-start.11 = (bf16[32,2048]{1,0:T(8,128)(2,1)S(1)}, bf16[32,2048]{1,0:T(8,128)(2,1)S(1)}, u32[]{:S(2)}, u32[]{:S(2)}) collective-permute-start(bf16[32,2048]{1,0:T(8,128)(2,1)S(1)} %collective-permute-done.9), channel_id=1, source_target_pairs={{0,15},{1,0},{2,1},{3,2},{4,3},{5,4},{6,5},{7,6},{8,7},{9,8},{10,9... | collective-permute-start | bytes 393224 | tf_op jit(solution)/shard_map/ppermute | solution.py:28
  236.4 4.4 %collective-permute-start.13 = (bf16[32,2048]{1,0:T(8,128)(2,1)S(1)}, bf16[32,2048]{1,0:T(8,128)(2,1)S(1)}, u32[]{:S(2)}, u32[]{:S(2)}) collective-permute-start(bf16[32,2048]{1,0:T(8,128)(2,1)S(1)} %collective-permute-done.11), channel_id=1, source_target_pairs={{0,15},{1,0},{2,1},{3,2},{4,3},{5,4},{6,5},{7,6},{8,7},{9,8},{10,9... | collective-permute-start | bytes 393224 | tf_op jit(solution)/shard_map/ppermute | solution.py:28
  244.8 5.7 %collective-permute-done.14 = bf16[32,2048]{1,0:T(8,128)(2,1)S(1)} collective-permute-done((bf16[32,2048]{1,0:T(8,128)(2,1)S(1)}, bf16[32,2048]{1,0:T(8,128)(2,1)S(1)}, u32[]{:S(2)}, u32[]{:S(2)}) %collective-permute-start.14) | collective-permute-done | bytes 131104 | tf_op jit(solution)/shard_map/ppermute | solution.py:23
  251.3 11.8 %reshape.40 = bf16[12288,3,32]{2,1,0:T(4,128)(2,1)} reshape(bf16[16,2,36864]{2,1,0:T(2,128)(2,1)S(1)} %all-to-all-done) | data formatting | bytes 4718592
  263.0 11.7 %copy.19 = bf16[3,32,16,768]{3,2,1,0:T(8,128)(2,1)S(1)} copy(bf16[3,32,16,768]{1,0,3,2:T(4,128)(2,1)} %bitcast.68) | data formatting | bytes 4718592 | tf_op jit(solution)/shard_map/all_to_all | solution.py:94
  275.6 3.4 %fusion.1 = bf16[1,768,2048]{1,2,0:T(8,128)(2,1)S(1)} fusion(bf16[512,2048]{1,0:T(8,128)(2,1)} %constant_dynamic-update-slice_fusion, bf16[512,768]{1,0:T(8,128)(2,1)S(1)} %bitcast.77), kind=kOutput, calls=%fused_computation.12 | convolution fusion | flops 1612185600 | bytes 6029312 | tf_op jit(solution)/shard_map/dot_general | solution.py:86
  279.0 3.4 %fusion.2 = bf16[1,768,2048]{1,2,0:T(8,128)(2,1)S(1)} fusion(bf16[512,2048]{1,0:T(8,128)(2,1)} %constant_dynamic-update-slice_fusion, bf16[512,768]{1,0:T(8,128)(2,1)S(1)} %bitcast.76), kind=kOutput, calls=%fused_computation.13 | convolution fusion | flops 1612185600 | bytes 6029312 | tf_op jit(solution)/shard_map/dot_general | solution.py:86
  282.5 3.4 %fusion = bf16[1,768,2048]{1,2,0:T(8,128)(2,1)S(1)} fusion(bf16[512,2048]{1,0:T(8,128)(2,1)} %constant_dynamic-update-slice_fusion, bf16[512,768]{1,0:T(8,128)(2,1)S(1)} %bitcast.75), kind=kOutput, calls=%fused_computation.11 | convolution fusion | flops 1612185600 | bytes 6029312 | tf_op jit(solution)/shard_map/dot_general | solution.py:86
  285.9 4.5 %pad_maximum_fusion = bf16[3,768,2048]{1,2,0:T(8,128)(2,1)} fusion(bf16[1,768,2048]{1,2,0:T(8,128)(2,1)S(1)} %fusion.2, bf16[1,768,2048]{1,2,0:T(8,128)(2,1)S(1)} %fusion.1, bf16[1,768,2048]{1,2,0:T(8,128)(2,1)S(1)} %fusion), kind=kLoop, calls=%fused_computation.7 | loop fusion | flops 9437184 | bytes 18874368 | tf_op jit(solution)/shard_map/stack | solution.py:90
  290.4 12.6 %copy.18 = bf16[3,768,2048]{2,1,0:T(8,128)(2,1)} copy(bf16[3,768,2048]{1,2,0:T(8,128)(2,1)} %pad_maximum_fusion) | data formatting | bytes 18874368 | tf_op jit(solution)/shard_map/stack | solution.py:90
  (170 shorter events, 39.7 us)
Async XLA Ops:
  31.0 7.6 %copy-start.5 = (f32[2048]{0:T(1024)S(1)}, f32[2048]{0:T(1024)}, u32[]{:S(2)}) copy-start(f32[2048]{0:T(1024)} %param.10) | copy-start | bytes 24580
  31.0 7.6 %copy-start.6 = (f32[2048]{0:T(1024)S(1)}, f32[2048]{0:T(1024)}, u32[]{:S(2)}) copy-start(f32[2048]{0:T(1024)} %param.11) | copy-start | bytes 24580
  31.0 7.6 %copy-start.1 = (f32[32,2048]{1,0:T(8,128)S(1)}, f32[32,2048]{1,0:T(8,128)}, u32[]{:S(2)}) copy-start(f32[32,2048]{1,0:T(8,128)} %param.8) | copy-start | bytes 786436
  31.0 7.6 %copy-start.7 = (f32[32]{0:T(128)S(1)}, f32[32]{0:T(128)}, u32[]{:S(2)}) copy-start(f32[32]{0:T(128)} %param.9) | copy-start | bytes 388
  31.0 220.3 %all-to-all-start = ((bf16[16,2,36864]{2,1,0:T(2,128)(2,1)}), bf16[16,2,36864]{2,1,0:T(2,128)(2,1)S(1)}, u32[]{:S(2)}, u32[]{:S(2)}) async-start(bf16[16,2,36864]{2,1,0:T(2,128)(2,1)} %reshape.39), calls=%async_computation | async-start | bytes 4718592 | tf_op jit(solution)/shard_map/all_to_all | solution.py:94
  41.9 2.9 copy-start.3
  44.9 2.1 copy-start
  47.0 47.5 %copy-start.2 = (f32[1,2048]{1,0:T(1,128)S(1)}, f32[1,2048]{1,0:T(1,128)}, u32[]{:S(2)}) copy-start(f32[1,2048]{1,0:T(1,128)} %slice.387) | copy-start | bytes 24580
  94.5 73.3 %copy-start.4 = (f32[2048]{0:T(1024)S(1)}, f32[2048]{0:T(1024)}, u32[]{:S(2)}) copy-start(f32[2048]{0:T(1024)} %param.12) | copy-start | bytes 24580
  170.1 30.4 %collective-permute-start = (bf16[32,2048]{1,0:T(8,128)(2,1)S(1)}, bf16[32,2048]{1,0:T(8,128)(2,1)S(1)}, u32[]{:S(2)}, u32[]{:S(2)}) collective-permute-start(bf16[32,2048]{1,0:T(8,128)(2,1)S(1)} %get-tuple-element.86), channel_id=1, source_target_pairs={{0,1},{1,2},{2,3},{3,4},{4,5},{5,6},{6,7},{7,8},{8,9},{9,10},{10,1... | collective-permute-start | bytes 393224 | tf_op jit(solution)/shard_map/ppermute | solution.py:23
  172.3 28.2 %collective-permute-start.1 = (bf16[32,2048]{1,0:T(8,128)(2,1)S(1)}, bf16[32,2048]{1,0:T(8,128)(2,1)S(1)}, u32[]{:S(2)}, u32[]{:S(2)}) collective-permute-start(bf16[32,2048]{1,0:T(8,128)(2,1)S(1)} %get-tuple-element.86), channel_id=1, source_target_pairs={{0,15},{1,0},{2,1},{3,2},{4,3},{5,4},{6,5},{7,6},{8,7},{9,8},{10,9... | collective-permute-start | bytes 393224 | tf_op jit(solution)/shard_map/ppermute | solution.py:28
  200.5 7.2 %collective-permute-start.2 = (bf16[32,2048]{1,0:T(8,128)(2,1)S(1)}, bf16[32,2048]{1,0:T(8,128)(2,1)S(1)}, u32[]{:S(2)}, u32[]{:S(2)}) collective-permute-start(bf16[32,2048]{1,0:T(8,128)(2,1)S(1)} %collective-permute-done), channel_id=1, source_target_pairs={{0,1},{1,2},{2,3},{3,4},{4,5},{5,6},{6,7},{7,8},{8,9},{9,10},{10,1... | collective-permute-start | bytes 393224 | tf_op jit(solution)/shard_map/ppermute | solution.py:23
  200.5 7.2 %collective-permute-start.3 = (bf16[32,2048]{1,0:T(8,128)(2,1)S(1)}, bf16[32,2048]{1,0:T(8,128)(2,1)S(1)}, u32[]{:S(2)}, u32[]{:S(2)}) collective-permute-start(bf16[32,2048]{1,0:T(8,128)(2,1)S(1)} %collective-permute-done.1), channel_id=1, source_target_pairs={{0,15},{1,0},{2,1},{3,2},{4,3},{5,4},{6,5},{7,6},{8,7},{9,8},{10,9... | collective-permute-start | bytes 393224 | tf_op jit(solution)/shard_map/ppermute | solution.py:28
  207.6 7.2 %collective-permute-start.4 = (bf16[32,2048]{1,0:T(8,128)(2,1)S(1)}, bf16[32,2048]{1,0:T(8,128)(2,1)S(1)}, u32[]{:S(2)}, u32[]{:S(2)}) collective-permute-start(bf16[32,2048]{1,0:T(8,128)(2,1)S(1)} %collective-permute-done.2), channel_id=1, source_target_pairs={{0,1},{1,2},{2,3},{3,4},{4,5},{5,6},{6,7},{7,8},{8,9},{9,10},{10,1... | collective-permute-start | bytes 393224 | tf_op jit(solution)/shard_map/ppermute | solution.py:23
  207.7 7.2 %collective-permute-start.5 = (bf16[32,2048]{1,0:T(8,128)(2,1)S(1)}, bf16[32,2048]{1,0:T(8,128)(2,1)S(1)}, u32[]{:S(2)}, u32[]{:S(2)}) collective-permute-start(bf16[32,2048]{1,0:T(8,128)(2,1)S(1)} %collective-permute-done.3), channel_id=1, source_target_pairs={{0,15},{1,0},{2,1},{3,2},{4,3},{5,4},{6,5},{7,6},{8,7},{9,8},{10,9... | collective-permute-start | bytes 393224 | tf_op jit(solution)/shard_map/ppermute | solution.py:28
  214.8 7.2 %collective-permute-start.6 = (bf16[32,2048]{1,0:T(8,128)(2,1)S(1)}, bf16[32,2048]{1,0:T(8,128)(2,1)S(1)}, u32[]{:S(2)}, u32[]{:S(2)}) collective-permute-start(bf16[32,2048]{1,0:T(8,128)(2,1)S(1)} %collective-permute-done.4), channel_id=1, source_target_pairs={{0,1},{1,2},{2,3},{3,4},{4,5},{5,6},{6,7},{7,8},{8,9},{9,10},{10,1... | collective-permute-start | bytes 393224 | tf_op jit(solution)/shard_map/ppermute | solution.py:23
  214.8 7.2 %collective-permute-start.7 = (bf16[32,2048]{1,0:T(8,128)(2,1)S(1)}, bf16[32,2048]{1,0:T(8,128)(2,1)S(1)}, u32[]{:S(2)}, u32[]{:S(2)}) collective-permute-start(bf16[32,2048]{1,0:T(8,128)(2,1)S(1)} %collective-permute-done.5), channel_id=1, source_target_pairs={{0,15},{1,0},{2,1},{3,2},{4,3},{5,4},{6,5},{7,6},{8,7},{9,8},{10,9... | collective-permute-start | bytes 393224 | tf_op jit(solution)/shard_map/ppermute | solution.py:28
  222.0 7.2 %collective-permute-start.8 = (bf16[32,2048]{1,0:T(8,128)(2,1)S(1)}, bf16[32,2048]{1,0:T(8,128)(2,1)S(1)}, u32[]{:S(2)}, u32[]{:S(2)}) collective-permute-start(bf16[32,2048]{1,0:T(8,128)(2,1)S(1)} %collective-permute-done.6), channel_id=1, source_target_pairs={{0,1},{1,2},{2,3},{3,4},{4,5},{5,6},{6,7},{7,8},{8,9},{9,10},{10,1... | collective-permute-start | bytes 393224 | tf_op jit(solution)/shard_map/ppermute | solution.py:23
  222.0 7.2 %collective-permute-start.9 = (bf16[32,2048]{1,0:T(8,128)(2,1)S(1)}, bf16[32,2048]{1,0:T(8,128)(2,1)S(1)}, u32[]{:S(2)}, u32[]{:S(2)}) collective-permute-start(bf16[32,2048]{1,0:T(8,128)(2,1)S(1)} %collective-permute-done.7), channel_id=1, source_target_pairs={{0,15},{1,0},{2,1},{3,2},{4,3},{5,4},{6,5},{7,6},{8,7},{9,8},{10,9... | collective-permute-start | bytes 393224 | tf_op jit(solution)/shard_map/ppermute | solution.py:28
  229.2 7.2 %collective-permute-start.10 = (bf16[32,2048]{1,0:T(8,128)(2,1)S(1)}, bf16[32,2048]{1,0:T(8,128)(2,1)S(1)}, u32[]{:S(2)}, u32[]{:S(2)}) collective-permute-start(bf16[32,2048]{1,0:T(8,128)(2,1)S(1)} %collective-permute-done.8), channel_id=1, source_target_pairs={{0,1},{1,2},{2,3},{3,4},{4,5},{5,6},{6,7},{7,8},{8,9},{9,10},{10,1... | collective-permute-start | bytes 393224 | tf_op jit(solution)/shard_map/ppermute | solution.py:23
  229.2 7.2 %collective-permute-start.11 = (bf16[32,2048]{1,0:T(8,128)(2,1)S(1)}, bf16[32,2048]{1,0:T(8,128)(2,1)S(1)}, u32[]{:S(2)}, u32[]{:S(2)}) collective-permute-start(bf16[32,2048]{1,0:T(8,128)(2,1)S(1)} %collective-permute-done.9), channel_id=1, source_target_pairs={{0,15},{1,0},{2,1},{3,2},{4,3},{5,4},{6,5},{7,6},{8,7},{9,8},{10,9... | collective-permute-start | bytes 393224 | tf_op jit(solution)/shard_map/ppermute | solution.py:28
  236.4 7.1 %collective-permute-start.12 = (bf16[32,2048]{1,0:T(8,128)(2,1)S(1)}, bf16[32,2048]{1,0:T(8,128)(2,1)S(1)}, u32[]{:S(2)}, u32[]{:S(2)}) collective-permute-start(bf16[32,2048]{1,0:T(8,128)(2,1)S(1)} %collective-permute-done.10), channel_id=1, source_target_pairs={{0,1},{1,2},{2,3},{3,4},{4,5},{5,6},{6,7},{7,8},{8,9},{9,10},{10,1... | collective-permute-start | bytes 393224 | tf_op jit(solution)/shard_map/ppermute | solution.py:23
  236.4 7.8 %collective-permute-start.13 = (bf16[32,2048]{1,0:T(8,128)(2,1)S(1)}, bf16[32,2048]{1,0:T(8,128)(2,1)S(1)}, u32[]{:S(2)}, u32[]{:S(2)}) collective-permute-start(bf16[32,2048]{1,0:T(8,128)(2,1)S(1)} %collective-permute-done.11), channel_id=1, source_target_pairs={{0,15},{1,0},{2,1},{3,2},{4,3},{5,4},{6,5},{7,6},{8,7},{9,8},{10,9... | collective-permute-start | bytes 393224 | tf_op jit(solution)/shard_map/ppermute | solution.py:28
  243.5 7.1 %collective-permute-start.14 = (bf16[32,2048]{1,0:T(8,128)(2,1)S(1)}, bf16[32,2048]{1,0:T(8,128)(2,1)S(1)}, u32[]{:S(2)}, u32[]{:S(2)}) collective-permute-start(bf16[32,2048]{1,0:T(8,128)(2,1)S(1)} %collective-permute-done.12), channel_id=1, source_target_pairs={{0,1},{1,2},{2,3},{3,4},{4,5},{5,6},{6,7},{7,8},{8,9},{9,10},{10,1... | collective-permute-start | bytes 393224 | tf_op jit(solution)/shard_map/ppermute | solution.py:23
